TPU v7x, 32 devices: a whole 2x2x4 slice. The times are simulated.
32 devices in a mesh: dom: 16 (over z, y, core), ch: 2 (over x).
Axes of the slice: x: 2, y: 2, z: 4, core: 2. Of those that a mesh axis runs over, the one named last changes fastest.
Arguments:
- node_irreps: bfloat16 [49, 128, 256], P(None, 'ch', 'dom'), may hold values from -6 to 6
- out_grad: bfloat16 [49, 128, 256], P(None, 'ch', 'dom'), may hold values from -6 to 6
- edge_source: int32 [8, 256], P(None, 'dom'), may hold values from 0 to 31
- edge_rotation: int32 [8, 256], P(None, 'dom'), may hold values from 0 to 255
- edge_count: int32 [256], P('dom'), may hold values from 1 to 8
- ghost_slot: int32 [256], P('dom'), may hold values from 0 to 15, as said below
- wigner: float32 [455, 4096], P(None, 'dom'), may hold values from -1 to 1, as said below
- so2_m0: bfloat16 [7, 128, 7, 128], P(None, 'ch'), may hold values from -0.1875 to 0.1875
- so2_m1: bfloat16 [2, 6, 128, 6, 128], P(None, None, 'ch'), may hold values from -0.15625 to 0.15625
- so2_m2: bfloat16 [2, 5, 128, 5, 128], P(None, None, 'ch'), may hold values from -0.15625 to 0.15625
- attn_vector: float32 [128], P('ch'), may hold values from -60 to 60
Outputs:
- updated: bfloat16 [49, 128, 256], P(None, 'ch', 'dom')
- irreps_grad: float32 [49, 128, 256], P(None, 'ch', 'dom')
Inputs may be any that keep to these rules, and one draw needn't show every extreme that they name: `edge_source`: slots below 16 are the domain's own atoms in order; slot 16 + g is the domain's ghost g. `edge_rotation`: picks one of the 256 columns of wigner that belong to the atom's domain. Slots j < edge_count[a] are live, the others padding. `ghost_slot`: of a domain's 16 entries, the first 8 name atoms of the previous domain (cyclically) among its last 16 slots, the others atoms of the next domain among its first 16 slots. `wigner`: each column holds for l = 0..6 an orthogonal (2l+1) x (2l+1) block, row-major, blocks in order of l.
All inputs are finite; a program needn't handle non-finite values.
Results may differ from a plain program's by a relative error of at most 0.012.
The roundings to bfloat16 on the way count: a program that leaves them out, or rounds other values in their place, can miss the bound.
Values may be sent and summed in bfloat16 or wider, within the bound.
A program may use at most 128 MiB of HBM per device.

v0:
```python
import functools

import jax
import jax.numpy as jnp
from jax import lax
from jax.experimental import pallas as pl
from jax.experimental.pallas import tpu as pltpu
from jax.sharding import PartitionSpec as P

HEADS = 8
LMAX = 6
MMAX = 2
CHUNK = 16
MESH = pl.DeviceIdType.MESH
VMEM = pltpu.VMEM
BF = jnp.bfloat16
F32 = jnp.float32


def degree_blocks():
    out = []
    offset = 0
    for level in range(LMAX + 1):
        width = 2 * level + 1
        reach = min(level, MMAX)
        out.append((level, width, offset, list(range(-reach, reach + 1))))
        offset += width * width
    return out


BLOCKS = degree_blocks()


def dot(a, b, dims):
    return lax.dot_general(a, b, (dims, ((), ())), preferred_element_type=F32)


def nn(a, b):
    return dot(a, b, ((1,), (0,)))


def nt(a, b):
    return dot(a, b, ((1,), (1,)))


def tn(a, b):
    return dot(a, b, ((0,), (0,)))


def iota(shape, dim):
    return lax.broadcasted_iota(jnp.int32, shape, dim)


def eye(n, dtype):
    return (iota((n, n), 0) == iota((n, n), 1)).astype(dtype)


def peers(n_dom, n_ch):
    return [(s, r, step) for s in range(n_ch) for r, step in ((0, 0), (1, -1), (2, 1)) if (s, r) != (0, 0)]


def greet(n_dom, n_ch):
    dom = lax.axis_index("dom")
    ch = lax.axis_index("ch")
    barrier = pltpu.get_barrier_semaphore()
    others = peers(n_dom, n_ch)
    for s, r, step in others:
        target = (lax.rem(dom + step + n_dom, n_dom), lax.rem(ch + s, n_ch))
        pl.semaphore_signal(barrier, inc=1, device_id=target, device_id_type=MESH)
    pl.semaphore_wait(barrier, len(others))
    return dom, ch


def share_kernel(n_dom, n_ch, node_ref, table_ref, own, send_sem, recv_sem, local_sem):
    count, group, atoms = node_ref.shape
    rows = node_ref[...].reshape(count * group, atoms)
    own[...] = nt(eye(atoms, BF), rows).astype(BF)
    dom, ch = greet(n_dom, n_ch)
    copies = []
    for s, r, step in peers(n_dom, n_ch):
        block = {0: 0, -1: 2, 1: 1}[step]
        copies.append(
            pltpu.make_async_remote_copy(
                src_ref=own,
                dst_ref=table_ref.at[ch, block],
                send_sem=send_sem.at[s, r],
                recv_sem=recv_sem.at[s, r],
                device_id=(lax.rem(dom + step + n_dom, n_dom), lax.rem(ch + s, n_ch)),
                device_id_type=MESH,
            )
        )
    for copy in copies:
        copy.start()
    mine = pltpu.make_async_copy(own, table_ref.at[ch, 0], local_sem)
    mine.start()
    mine.wait()
    for copy in copies:
        copy.wait()


def return_kernel(n_dom, n_ch, grads_ref, cot_ref, out_ref, landed, send_sem, recv_sem, local_sem):
    count, group, atoms = cot_ref.shape
    dom, ch = greet(n_dom, n_ch)
    copies = []
    for s, r, step in peers(n_dom, n_ch):
        other = lax.rem(ch + s, n_ch)
        copies.append(
            pltpu.make_async_remote_copy(
                src_ref=grads_ref.at[other, r],
                dst_ref=landed.at[ch, r],
                send_sem=send_sem.at[s, r],
                recv_sem=recv_sem.at[s, r],
                device_id=(lax.rem(dom + step + n_dom, n_dom), other),
                device_id_type=MESH,
            )
        )
    for copy in copies:
        copy.start()
    mine = pltpu.make_async_copy(grads_ref.at[ch, 0], landed.at[ch, 0], local_sem)
    mine.start()
    mine.wait()
    for copy in copies:
        copy.wait()
    total = n_ch * 3 * atoms
    terms = landed[...].reshape(total, count * group)
    pick = (lax.rem(iota((total, atoms), 0), atoms) == iota((total, atoms), 1)).astype(BF)
    summed = tn(terms, pick)
    out_ref[...] = cot_ref[...].astype(F32) + summed.reshape(count, group, atoms)


def roll_all(x, atoms, op):
    shift = atoms
    while shift < x.shape[1]:
        x = op(x, pltpu.roll(x, shift, 1))
        shift *= 2
    return x


def per_head(x, head):
    group, edges = x.shape
    total = jnp.sum(x.reshape(group // head, head, edges), axis=1, keepdims=True)
    return jnp.broadcast_to(total, (group // head, head, edges)).reshape(group, edges)


def work_kernel(
    head,
    table_ref,
    node_ref,
    cot_ref,
    source_ref,
    turn_ref,
    live_ref,
    ghost_ref,
    wig_ref,
    w0_ref,
    w1_ref,
    w2_ref,
    attn_ref,
    updated_ref,
    grads_ref,
    turned,
    feats,
    rot0,
    rot1,
    rot2,
    y_ref,
    cots,
    gy_ref,
    agg_ref,
):
    n_ch, _, atoms, width_all = table_ref.shape
    count, group, _ = node_ref.shape
    chans = n_ch * group
    slots = source_ref.shape[0]
    edges = slots * atoms
    rows = count * group
    rots = wig_ref.shape[1]

    spread_f = (lax.rem(iota((atoms, edges), 1), atoms) == iota((atoms, edges), 0)).astype(BF)
    mine = lax.div(iota((slots, edges), 1), atoms) == iota((slots, edges), 0)

    def lanes(ref):
        wide = nn(ref[...].astype(F32).astype(BF), spread_f)
        return jnp.sum(jnp.where(mine, wide, 0.0), axis=0, keepdims=True).astype(jnp.int32)

    source = lanes(source_ref)
    turn = lanes(turn_ref)
    counts = nn(jnp.broadcast_to(live_ref[...], (8, atoms)).astype(F32).astype(BF), spread_f)[:1]
    n_ghost = ghost_ref.shape[1]
    ghost_col = jnp.sum(
        eye(n_ghost, F32) * ghost_ref[...].astype(F32), axis=1, keepdims=True
    )
    picked = iota((n_ghost, edges), 0) == source - atoms
    ghost = jnp.sum(jnp.where(picked, ghost_col, 0.0), axis=0, keepdims=True).astype(jnp.int32)
    raw = jnp.where(
        source < atoms,
        source,
        jnp.where(source < atoms + n_ghost // 2, ghost + atoms, ghost + 2 * atoms),
    )
    pick = (iota((3 * atoms, edges), 0) == raw).astype(F32).astype(BF)
    pick_turn = (iota((rots, edges), 0) == turn).astype(F32).astype(BF)

    wig = wig_ref[...]
    high = wig.astype(BF)
    low = (wig - high.astype(F32)).astype(BF)
    turned[...] = nn(high, pick_turn) + nn(low, pick_turn)

    def coef(offset, width, row, col):
        at = offset + row * width + col
        return turned[at : at + 1, :]

    for p in range(n_ch):
        feats[p * rows : (p + 1) * rows, :] = tn(
            table_ref[p].reshape(3 * atoms, width_all), pick
        )
    cots[...] = nn(cot_ref[...].reshape(rows, atoms), spread_f)

    per = group // CHUNK

    def rot_slot(level, order, at, n):
        if order == 0:
            return 0, level * n + at, 0
        first = (level - abs(order)) * n + at
        return abs(order), first, 0 if order > 0 else edges

    rot_refs = (rot0, rot1, rot2)

    def rotate_in(i, carry):
        base = pl.multiple_of(lax.div(i, per) * rows + lax.rem(i, per) * CHUNK, CHUNK)
        at = pl.multiple_of(i * CHUNK, CHUNK)
        for level, width, offset, kept in BLOCKS:
            f = [
                feats[pl.ds(base + (level * level + q) * group, CHUNK), :] for q in range(width)
            ]
            for order in kept:
                acc = coef(offset, width, level + order, 0) * f[0]
                for q in range(1, width):
                    acc = acc + coef(offset, width, level + order, q) * f[q]
                which, row, lane = rot_slot(level, order, at, chans)
                rot_refs[which][pl.ds(row, CHUNK), lane : lane + edges] = acc.astype(BF)
        return carry

    lax.fori_loop(0, chans // CHUNK, rotate_in, 0)

    y_at = {}
    pos = 0
    for level in range(LMAX + 1):
        y_at[(level, 0)] = pos
        pos += group
    y_ref[0:pos, :] = nn(w0_ref[...], rot0[...])
    for order, w_ref, rot in ((1, w1_ref, rot1), (2, w2_ref, rot2)):
        n = (LMAX + 1 - order) * group
        both = nn(w_ref[...], rot[...])
        y_ref[pos : pos + n, :] = both[:n, :edges] - both[n:, edges:]
        y_ref[pos + n : pos + 2 * n, :] = both[:n, edges:] + both[n:, :edges]
        for level in range(order, LMAX + 1):
            y_at[(level, order)] = pos + (level - order) * group
            y_at[(level, -order)] = pos + n + (level - order) * group
        pos += 2 * n

    scalar = y_ref[0:group, :]
    sig = jax.nn.sigmoid(scalar)
    attn = jnp.sum(eye(group, F32) * attn_ref[...], axis=1, keepdims=True)
    score = per_head(scalar * sig * attn, head)
    live = lax.div(iota((group, edges), 1), atoms).astype(F32) < counts
    top = roll_all(jnp.where(live, score, -1e30), atoms, jnp.maximum)
    weight = jnp.exp(jnp.where(live, score - top, -1e30))
    weight = weight / roll_all(weight, atoms, jnp.add)

    gate = sig * weight
    proj = []
    for c in range(group // CHUNK):
        at = c * CHUNK
        gate_c = gate[at : at + CHUNK]
        total = jnp.zeros((CHUNK, edges), F32)
        for level, width, offset, kept in BLOCKS:
            ys = [y_ref[y_at[(level, o)] + at : y_at[(level, o)] + at + CHUNK, :] for o in kept]
            vs = [y * gate_c for y in ys]
            gs = [None] * len(kept)
            for q in range(width):
                k = (level * level + q) * group + at
                g = cots[k : k + CHUNK, :]
                acc = None
                for j, order in enumerate(kept):
                    d = coef(offset, width, level + order, q)
                    term = d * vs[j]
                    acc = term if acc is None else acc + term
                    back = d * g
                    gs[j] = back if gs[j] is None else gs[j] + back
                agg_ref[k : k + CHUNK, :] = acc.astype(BF)
            for j, order in enumerate(kept):
                total = total + gs[j] * ys[j]
                if (level, order) == (0, 0):
                    continue
                row = y_at[(level, order)] + at
                gy_ref[row : row + CHUNK, :] = (gs[j] * gate_c).astype(BF)
            if level == 0:
                first = gs[0] * gate_c
        proj.append((total, first))
    total = jnp.concatenate([t for t, _ in proj], axis=0)
    first = jnp.concatenate([f for _, f in proj], axis=0)
    dweight = per_head(sig * total, head)
    dscore = weight * (dweight - roll_all(weight * dweight, atoms, jnp.add))
    slope = sig * (1.0 - sig)
    first = first + weight * total * slope + dscore * attn * (sig + scalar * slope)
    gy_ref[0:group, :] = first.astype(BF)

    agg = nt(agg_ref[...], spread_f).reshape(count, group, atoms)
    updated_ref[...] = (node_ref[...].astype(F32) + agg).astype(BF)

    n0 = (LMAX + 1) * group
    rot0[...] = tn(w0_ref[...], gy_ref[0:n0, :]).astype(BF)
    pos = n0
    for order, w_ref, rot in ((1, w1_ref, rot1), (2, w2_ref, rot2)):
        n = (LMAX + 1 - order) * group
        plus = gy_ref[pos : pos + n, :]
        minus = gy_ref[pos + n : pos + 2 * n, :]
        both = jnp.concatenate(
            [jnp.concatenate([plus, minus], axis=1), jnp.concatenate([minus, -plus], axis=1)],
            axis=0,
        )
        rot[...] = tn(w_ref[...], both).astype(BF)
        pos += 2 * n

    def rotate_out(i, carry):
        base = pl.multiple_of(lax.div(i, per) * rows + lax.rem(i, per) * CHUNK, CHUNK)
        at = pl.multiple_of(i * CHUNK, CHUNK)
        for level, width, offset, kept in BLOCKS:
            ds = []
            for order in kept:
                which, row, lane = rot_slot(level, order, at, chans)
                ds.append(
                    rot_refs[which][pl.ds(row, CHUNK), lane : lane + edges].astype(F32)
                )
            for q in range(width):
                acc = None
                for j, order in enumerate(kept):
                    term = coef(offset, width, level + order, q) * ds[j]
                    acc = term if acc is None else acc + term
                feats[pl.ds(base + (level * level + q) * group, CHUNK), :] = acc
        return carry

    lax.fori_loop(0, chans // CHUNK, rotate_out, 0)
    for p in range(n_ch):
        part = feats[p * rows : (p + 1) * rows, :].astype(BF)
        grads_ref[p] = nt(pick, part).astype(BF).reshape(3, atoms, width_all)


def on_device(
    n_dom,
    n_ch,
    node_irreps,
    out_grad,
    edge_source,
    edge_rotation,
    edge_count,
    ghost_slot,
    wigner,
    so2_m0,
    so2_m1,
    so2_m2,
    attn_vector,
):
    count, group, atoms = node_irreps.shape
    chans = n_ch * group
    slots = edge_source.shape[0]
    edges = slots * atoms
    rows = count * group
    vmem = pl.BlockSpec(memory_space=VMEM)
    blocks = jax.ShapeDtypeStruct((n_ch, 3, atoms, rows), BF)
    sems = [
        pltpu.SemaphoreType.DMA((n_ch, 3)),
        pltpu.SemaphoreType.DMA((n_ch, 3)),
        pltpu.SemaphoreType.DMA,
    ]
    table = pl.pallas_call(
        functools.partial(share_kernel, n_dom, n_ch),
        out_shape=blocks,
        in_specs=[vmem],
        out_specs=vmem,
        scratch_shapes=[VMEM((atoms, rows), BF)] + sems,
        compiler_params=pltpu.CompilerParams(collective_id=0, has_side_effects=True),
        name="share",
    )(node_irreps)
    n_pairs = sum(len(b[3]) for b in BLOCKS)
    updated, grads = pl.pallas_call(
        functools.partial(work_kernel, chans // HEADS),
        out_shape=(jax.ShapeDtypeStruct(node_irreps.shape, BF), blocks),
        in_specs=[vmem] * 12,
        out_specs=(vmem, vmem),
        scratch_shapes=[
            VMEM((wigner.shape[0], edges), F32),
            VMEM((n_ch * rows, edges), F32),
            VMEM(((LMAX + 1) * chans, edges), BF),
            VMEM((LMAX * chans, 2 * edges), BF),
            VMEM(((LMAX - 1) * chans, 2 * edges), BF),
            VMEM((n_pairs * group, edges), F32),
            VMEM((rows, edges), F32),
            VMEM((n_pairs * group, edges), BF),
            VMEM((rows, edges), BF),
        ],
        compiler_params=pltpu.CompilerParams(vmem_limit_bytes=56 * 1024 * 1024),
        name="work",
    )(
        table,
        node_irreps,
        out_grad,
        edge_source,
        edge_rotation,
        edge_count.reshape(1, atoms),
        ghost_slot.reshape(1, -1),
        wigner,
        so2_m0.reshape((LMAX + 1) * group, (LMAX + 1) * chans),
        so2_m1.reshape(2 * LMAX * group, LMAX * chans),
        so2_m2.reshape(2 * (LMAX - 1) * group, (LMAX - 1) * chans),
        attn_vector.reshape(1, group),
    )
    irreps_grad = pl.pallas_call(
        functools.partial(return_kernel, n_dom, n_ch),
        out_shape=jax.ShapeDtypeStruct(node_irreps.shape, F32),
        in_specs=[vmem, vmem],
        out_specs=vmem,
        scratch_shapes=[VMEM(blocks.shape, BF)] + sems,
        compiler_params=pltpu.CompilerParams(collective_id=1, has_side_effects=True),
        name="give_back",
    )(grads, out_grad)
    return (updated, irreps_grad)


def solution(mesh):
    placed = (
        P(None, "ch", "dom"),
        P(None, "ch", "dom"),
        P(None, "dom"),
        P(None, "dom"),
        P("dom"),
        P("dom"),
        P(None, "dom"),
        P(None, "ch", None, None),
        P(None, None, "ch", None, None),
        P(None, None, "ch", None, None),
        P("ch"),
    )
    return jax.shard_map(
        functools.partial(on_device, mesh.shape["dom"], mesh.shape["ch"]),
        mesh=mesh,
        in_specs=placed,
        out_specs=(P(None, "ch", "dom"), P(None, "ch", "dom")),
        check_vma=False,
    )
```

profile of v0, /device:TPU:0, one launch (start us, length us, event | category | flops | bytes accessed | tf_op | source)
XLA Modules:
  0.0 51.4 jit_solution(9226936388336487443)
XLA Ops:
  0.6 0.0 copy-start.4
  0.6 2.2 %copy.22.node_ref = bf16[49,64,16]{2,1,0:T(8,128)(2,1)} copy(bf16[49,64,16]{1,2,0:T(8,128)(2,1)} %param.11) | data formatting | bytes 200704 | tf_op args[0]
  2.8 0.0 copy-start
  2.8 13.8 %share.1.table_ref = bf16[2,3,16,3136]{3,2,1,0:T(8,128)(2,1)} custom-call(bf16[49,64,16]{2,1,0:T(8,128)(2,1)} %copy.22.node_ref), custom_call_target="tpu_custom_call" | custom-call | tf_op jit(solution)/shard_map/share/pallas_call | solution.py:376
  16.6 0.0 copy-done.4
  16.6 1.2 %copy.27.cot_ref = bf16[49,64,16]{2,1,0:T(8,128)(2,1)} copy(bf16[49,64,16]{1,2,0:T(8,128)(2,1)S(1)} %copy-done.4) | data formatting | bytes 200704 | tf_op args[1]
  17.9 0.0 copy-done
  17.9 0.9 %copy.24 = bf16[2,6,64,6,128]{4,3,2,1,0:T(8,128)(2,1)S(1)} copy(bf16[2,6,64,6,128]{4,2,3,1,0:T(8,128)(2,1)S(1)} %copy-done) | data formatting | bytes 2359296 | tf_op args[8]
  18.8 0.0 copy-start.1
  18.8 1.2 %copy.37 = bf16[96,8,6,128]{3,1,2,0:T(8,128)(2,1)} copy(bf16[96,8,6,128]{3,2,1,0:T(8,128)(2,1)S(1)} %bitcast.18) | data formatting | bytes 2359296
  20.0 0.0 copy-done.1
  20.0 0.6 %copy.25 = bf16[2,5,64,5,128]{4,3,2,1,0:T(8,128)(2,1)S(1)} copy(bf16[2,5,64,5,128]{4,2,3,1,0:T(8,128)(2,1)S(1)} %copy-done.1) | data formatting | bytes 1638400 | tf_op args[9]
  20.6 0.0 copy-start.3
  20.6 1.1 %copy.38 = bf16[80,8,5,128]{3,1,2,0:T(8,128)(2,1)} copy(bf16[80,8,5,128]{3,2,1,0:T(8,128)(2,1)S(1)} %bitcast.19) | data formatting | bytes 1638400
  21.7 0.2 copy-done.3
  21.9 0.6 %copy.23 = bf16[7,64,7,128]{3,2,1,0:T(8,128)(2,1)S(1)} copy(bf16[7,64,7,128]{3,1,2,0:T(8,128)(2,1)S(1)} %copy-done.3) | data formatting | bytes 1605632 | tf_op args[7]
  22.5 1.0 %copy.39 = bf16[56,8,7,128]{3,1,2,0:T(8,128)(2,1)} copy(bf16[56,8,7,128]{3,2,1,0:T(8,128)(2,1)S(1)} %bitcast.21) | data formatting | bytes 1605632
  23.5 10.7 %work.1 = (bf16[49,64,16]{2,1,0:T(8,128)(2,1)}, bf16[2,3,16,3136]{3,2,1,0:T(8,128)(2,1)}) custom-call(bf16[2,3,16,3136]{3,2,1,0:T(8,128)(2,1)} %share.1.table_ref, bf16[49,64,16]{2,1,0:T(8,128)(2,1)} %copy.22.node_ref, bf16[49,64,16]{2,1,0:T(8,128)(2,1)} %copy.27.cot_ref, s32[8,16]{1,0:T(8,128)} %source_ref.1, s32[8,16]{1,0:T(8,128)} %turn_ref.1, ...), custom_call_target="tpu_custom_call" | custom-call | tf_op jit(solution)/shard_map/work/pallas_call | solution.py:386
  34.2 13.5 %give_back.1 = f32[49,64,16]{2,1,0:T(8,128)} custom-call(bf16[2,3,16,3136]{3,2,1,0:T(8,128)(2,1)} %get-tuple-element.5.grads_ref, bf16[49,64,16]{2,1,0:T(8,128)(2,1)} %copy.27.cot_ref), custom_call_target="tpu_custom_call" | custom-call | tf_op jit(solution)/shard_map/give_back/pallas_call | solution.py:418
  47.7 0.0 copy-start.2
  47.7 2.7 %copy.30 = f32[49,64,16]{1,2,0:T(8,128)} copy(f32[49,64,16]{2,1,0:T(8,128)} %give_back.1) | data formatting | bytes 401408
  50.4 0.0 copy-done.2
  50.4 1.0 %copy.29 = bf16[49,64,16]{1,2,0:T(8,128)(2,1)} copy(bf16[49,64,16]{2,1,0:T(8,128)(2,1)S(1)} %copy-done.2) | data formatting | bytes 200704
Async XLA Ops:
  0.6 16.0 %copy-start.4 = (bf16[49,64,16]{1,2,0:T(8,128)(2,1)S(1)}, bf16[49,64,16]{1,2,0:T(8,128)(2,1)}, u32[]{:S(2)}) copy-start(bf16[49,64,16]{1,2,0:T(8,128)(2,1)} %param.12) | copy-start | bytes 301060
  2.8 15.1 %copy-start = (bf16[2,6,64,6,128]{4,2,3,1,0:T(8,128)(2,1)S(1)}, bf16[2,6,64,6,128]{4,2,3,1,0:T(8,128)(2,1)}, u32[]{:S(2)}) copy-start(bf16[2,6,64,6,128]{4,2,3,1,0:T(8,128)(2,1)} %param.19) | copy-start | bytes 3538948
  18.8 1.2 %copy-start.1 = (bf16[2,5,64,5,128]{4,2,3,1,0:T(8,128)(2,1)S(1)}, bf16[2,5,64,5,128]{4,2,3,1,0:T(8,128)(2,1)}, u32[]{:S(2)}) copy-start(bf16[2,5,64,5,128]{4,2,3,1,0:T(8,128)(2,1)} %param.20) | copy-start | bytes 2457604
  20.6 1.3 %copy-start.3 = (bf16[7,64,7,128]{3,1,2,0:T(8,128)(2,1)S(1)}, bf16[7,64,7,128]{3,1,2,0:T(8,128)(2,1)}, u32[]{:S(2)}) copy-start(bf16[7,64,7,128]{3,1,2,0:T(8,128)(2,1)} %param.18) | copy-start | bytes 2408452
  47.7 2.7 %copy-start.2 = (bf16[49,64,16]{2,1,0:T(8,128)(2,1)S(1)}, bf16[49,64,16]{2,1,0:T(8,128)(2,1)}, u32[]{:S(2)}) copy-start(bf16[49,64,16]{2,1,0:T(8,128)(2,1)} %get-tuple-element.8) | copy-start | bytes 301060
where the time goes:
time: 51.6 us; the launch traced here: 51.4 us
  Pallas kernels  38 us (74%)
  local copies, waits for them, and re-layouts  12.7 us (25%)
  between operations  0.7 us (1%)
    pallas_call x1, Pallas kernels, on_device(): pl.pallas_call(functools.partial(share_kernel, n_dom, n_ch), out_shape=bl...  13.8 us
    pallas_call x1, Pallas kernels, on_device(): pl.pallas_call(functools.partial(return_kernel, n_dom, n_ch), out_shape=j...  13.5 us
    unnamed x20, local copies, waits for them, and re-layouts  12.7 us
    pallas_call x1, Pallas kernels, on_device(): pl.pallas_call(functools.partial(work_kernel, chans // HEADS), out_shape=...  10.7 us

commit v1 on v0

--- a/solution.py
+++ b/solution.py
@@ -55,79 +55,6 @@
     return (iota((n, n), 0) == iota((n, n), 1)).astype(dtype)
 
 
-def peers(n_dom, n_ch):
-    return [(s, r, step) for s in range(n_ch) for r, step in ((0, 0), (1, -1), (2, 1)) if (s, r) != (0, 0)]
-
-
-def greet(n_dom, n_ch):
-    dom = lax.axis_index("dom")
-    ch = lax.axis_index("ch")
-    barrier = pltpu.get_barrier_semaphore()
-    others = peers(n_dom, n_ch)
-    for s, r, step in others:
-        target = (lax.rem(dom + step + n_dom, n_dom), lax.rem(ch + s, n_ch))
-        pl.semaphore_signal(barrier, inc=1, device_id=target, device_id_type=MESH)
-    pl.semaphore_wait(barrier, len(others))
-    return dom, ch
-
-
-def share_kernel(n_dom, n_ch, node_ref, table_ref, own, send_sem, recv_sem, local_sem):
-    count, group, atoms = node_ref.shape
-    rows = node_ref[...].reshape(count * group, atoms)
-    own[...] = nt(eye(atoms, BF), rows).astype(BF)
-    dom, ch = greet(n_dom, n_ch)
-    copies = []
-    for s, r, step in peers(n_dom, n_ch):
-        block = {0: 0, -1: 2, 1: 1}[step]
-        copies.append(
-            pltpu.make_async_remote_copy(
-                src_ref=own,
-                dst_ref=table_ref.at[ch, block],
-                send_sem=send_sem.at[s, r],
-                recv_sem=recv_sem.at[s, r],
-                device_id=(lax.rem(dom + step + n_dom, n_dom), lax.rem(ch + s, n_ch)),
-                device_id_type=MESH,
-            )
-        )
-    for copy in copies:
-        copy.start()
-    mine = pltpu.make_async_copy(own, table_ref.at[ch, 0], local_sem)
-    mine.start()
-    mine.wait()
-    for copy in copies:
-        copy.wait()
-
-
-def return_kernel(n_dom, n_ch, grads_ref, cot_ref, out_ref, landed, send_sem, recv_sem, local_sem):
-    count, group, atoms = cot_ref.shape
-    dom, ch = greet(n_dom, n_ch)
-    copies = []
-    for s, r, step in peers(n_dom, n_ch):
-        other = lax.rem(ch + s, n_ch)
-        copies.append(
-            pltpu.make_async_remote_copy(
-                src_ref=grads_ref.at[other, r],
-                dst_ref=landed.at[ch, r],
-                send_sem=send_sem.at[s, r],
-                recv_sem=recv_sem.at[s, r],
-                device_id=(lax.rem(dom + step + n_dom, n_dom), other),
-                device_id_type=MESH,
-            )
-        )
-    for copy in copies:
-        copy.start()
-    mine = pltpu.make_async_copy(grads_ref.at[ch, 0], landed.at[ch, 0], local_sem)
-    mine.start()
-    mine.wait()
-    for copy in copies:
-        copy.wait()
-    total = n_ch * 3 * atoms
-    terms = landed[...].reshape(total, count * group)
-    pick = (lax.rem(iota((total, atoms), 0), atoms) == iota((total, atoms), 1)).astype(BF)
-    summed = tn(terms, pick)
-    out_ref[...] = cot_ref[...].astype(F32) + summed.reshape(count, group, atoms)
-
-
 def roll_all(x, atoms, op):
     shift = atoms
     while shift < x.shape[1]:
@@ -142,22 +69,35 @@
     return jnp.broadcast_to(total, (group // head, head, edges)).reshape(group, edges)
 
 
-def work_kernel(
+def kernel(
+    n_dom,
+    n_ch,
     head,
-    table_ref,
     node_ref,
-    cot_ref,
     source_ref,
     turn_ref,
     live_ref,
     ghost_ref,
+    attn_ref,
+    cot_hbm,
+    wig_hbm,
+    w0_hbm,
+    w1_hbm,
+    w2_hbm,
+    updated_ref,
+    out_ref,
+    cot_ref,
     wig_ref,
-    w0_ref,
-    w1_ref,
-    w2_ref,
-    attn_ref,
-    updated_ref,
+    w0,
+    w1,
+    w2,
+    table_ref,
     grads_ref,
+    landed,
+    sums,
+    partial,
+    flat,
+    flat_cot,
     turned,
     feats,
     rot0,
@@ -167,14 +107,73 @@
     cots,
     gy_ref,
     agg_ref,
+    dfeats,
+    load_sem,
+    table_sem,
+    ring_sem,
+    back_sem,
+    sum_sem,
 ):
-    n_ch, _, atoms, width_all = table_ref.shape
-    count, group, _ = node_ref.shape
+    count, atoms, group = node_ref.shape
     chans = n_ch * group
     slots = source_ref.shape[0]
     edges = slots * atoms
     rows = count * group
     rots = wig_ref.shape[1]
+    dom = lax.axis_index("dom")
+    ch = lax.axis_index("ch")
+    lower = lax.rem(dom + n_dom - 1, n_dom)
+    upper = lax.rem(dom + 1, n_dom)
+
+    load_cot = pltpu.make_async_copy(cot_hbm, cot_ref, load_sem.at[0])
+    load_wig = pltpu.make_async_copy(wig_hbm, wig_ref, load_sem.at[1])
+    load_wig.start()
+    load_cot.start()
+    load_w = []
+    for hbm, ref in ((w0_hbm, w0), (w1_hbm, w1), (w2_hbm, w2)):
+        for level in range(hbm.shape[-3]):
+            lanes_of = slice(level * chans, (level + 1) * chans)
+            if hbm.ndim == 4:
+                one, place = hbm.at[:, level], ref.at[:, :, lanes_of]
+            else:
+                one, place = hbm.at[:, :, level], ref.at[:, :, :, lanes_of]
+            load_w.append(pltpu.make_async_copy(one, place, load_sem.at[2 + len(load_w)]))
+            load_w[-1].start()
+
+    for k in range(count):
+        table_ref[ch, 0, :, k * group : (k + 1) * group] = node_ref[k]
+
+    def remote(source, target, sems, place, device):
+        return pltpu.make_async_remote_copy(
+            src_ref=source,
+            dst_ref=target,
+            send_sem=sems.at[(0,) + place],
+            recv_sem=sems.at[(1,) + place],
+            device_id=device,
+            device_id_type=MESH,
+        )
+
+    barrier = pltpu.get_barrier_semaphore()
+    partners = [(dom, lax.rem(ch + s, n_ch)) for s in range(1, n_ch)]
+    for target in [(lower, ch), (upper, ch)] + partners:
+        pl.semaphore_signal(barrier, inc=1, device_id=target, device_id_type=MESH)
+    pl.semaphore_wait(barrier, n_ch + 1)
+
+    own = table_ref.at[ch, 0]
+    across = [remote(own, own, table_sem, (s,), partners[s - 1]) for s in range(1, n_ch)]
+    for copy in across:
+        copy.start()
+
+    def pass_on(q, s):
+        both = [
+            remote(table_ref.at[q, 0], table_ref.at[q, 2], ring_sem, (s, 0), (lower, ch)),
+            remote(table_ref.at[q, 0], table_ref.at[q, 1], ring_sem, (s, 1), (upper, ch)),
+        ]
+        for copy in both:
+            copy.start()
+        return both
+
+    along = pass_on(ch, 0)
 
     spread_f = (lax.rem(iota((atoms, edges), 1), atoms) == iota((atoms, edges), 0)).astype(BF)
     mine = lax.div(iota((slots, edges), 1), atoms) == iota((slots, edges), 0)
@@ -200,6 +199,7 @@
     pick = (iota((3 * atoms, edges), 0) == raw).astype(F32).astype(BF)
     pick_turn = (iota((rots, edges), 0) == turn).astype(F32).astype(BF)
 
+    load_wig.wait()
     wig = wig_ref[...]
     high = wig.astype(BF)
     low = (wig - high.astype(F32)).astype(BF)
@@ -209,11 +209,21 @@
         at = offset + row * width + col
         return turned[at : at + 1, :]
 
+    for s in range(1, n_ch):
+        across[s - 1].wait_recv()
+        along += pass_on(lax.rem(ch + n_ch - s, n_ch), s)
+
+    load_cot.wait()
+    for k in range(count):
+        flat_cot[:, k * group : (k + 1) * group] = cot_ref[k]
+    cots[...] = tn(flat_cot[...], spread_f)
+
+    for copy in along:
+        copy.wait_recv()
     for p in range(n_ch):
         feats[p * rows : (p + 1) * rows, :] = tn(
-            table_ref[p].reshape(3 * atoms, width_all), pick
+            table_ref[p].reshape(3 * atoms, rows), pick
         )
-    cots[...] = nn(cot_ref[...].reshape(rows, atoms), spread_f)
 
     per = group // CHUNK
 
@@ -242,15 +252,20 @@
 
     lax.fori_loop(0, chans // CHUNK, rotate_in, 0)
 
+    for copy in load_w:
+        copy.wait()
+    w0_ref = w0[...].reshape((LMAX + 1) * group, (LMAX + 1) * chans)
+    w1_ref = w1[...].reshape(2 * LMAX * group, LMAX * chans)
+    w2_ref = w2[...].reshape(2 * (LMAX - 1) * group, (LMAX - 1) * chans)
     y_at = {}
     pos = 0
     for level in range(LMAX + 1):
         y_at[(level, 0)] = pos
         pos += group
-    y_ref[0:pos, :] = nn(w0_ref[...], rot0[...])
+    y_ref[0:pos, :] = nn(w0_ref, rot0[...])
     for order, w_ref, rot in ((1, w1_ref, rot1), (2, w2_ref, rot2)):
         n = (LMAX + 1 - order) * group
-        both = nn(w_ref[...], rot[...])
+        both = nn(w_ref, rot[...])
         y_ref[pos : pos + n, :] = both[:n, :edges] - both[n:, edges:]
         y_ref[pos + n : pos + 2 * n, :] = both[:n, edges:] + both[n:, :edges]
         for level in range(order, LMAX + 1):
@@ -305,11 +320,8 @@
     first = first + weight * total * slope + dscore * attn * (sig + scalar * slope)
     gy_ref[0:group, :] = first.astype(BF)
 
-    agg = nt(agg_ref[...], spread_f).reshape(count, group, atoms)
-    updated_ref[...] = (node_ref[...].astype(F32) + agg).astype(BF)
-
     n0 = (LMAX + 1) * group
-    rot0[...] = tn(w0_ref[...], gy_ref[0:n0, :]).astype(BF)
+    rot0[...] = tn(w0_ref, gy_ref[0:n0, :]).astype(BF)
     pos = n0
     for order, w_ref, rot in ((1, w1_ref, rot1), (2, w2_ref, rot2)):
         n = (LMAX + 1 - order) * group
@@ -319,12 +331,12 @@
             [jnp.concatenate([plus, minus], axis=1), jnp.concatenate([minus, -plus], axis=1)],
             axis=0,
         )
-        rot[...] = tn(w_ref[...], both).astype(BF)
+        rot[...] = tn(w_ref, both).astype(BF)
         pos += 2 * n
 
-    def rotate_out(i, carry):
-        base = pl.multiple_of(lax.div(i, per) * rows + lax.rem(i, per) * CHUNK, CHUNK)
-        at = pl.multiple_of(i * CHUNK, CHUNK)
+    def rotate_out(p, i, carry):
+        base = pl.multiple_of(i * CHUNK, CHUNK)
+        at = pl.multiple_of(p * group + i * CHUNK, CHUNK)
         for level, width, offset, kept in BLOCKS:
             ds = []
             for order in kept:
@@ -337,13 +349,50 @@
                 for j, order in enumerate(kept):
                     term = coef(offset, width, level + order, q) * ds[j]
                     acc = term if acc is None else acc + term
-                feats[pl.ds(base + (level * level + q) * group, CHUNK), :] = acc
+                dfeats[pl.ds(base + (level * level + q) * group, CHUNK), :] = acc.astype(BF)
         return carry
 
-    lax.fori_loop(0, chans // CHUNK, rotate_out, 0)
-    for p in range(n_ch):
-        part = feats[p * rows : (p + 1) * rows, :].astype(BF)
-        grads_ref[p] = nt(pick, part).astype(BF).reshape(3, atoms, width_all)
+    homeward = []
+    for s in list(range(1, n_ch)) + [0]:
+        p = lax.rem(ch + s, n_ch)
+        lax.fori_loop(0, per, functools.partial(rotate_out, p), 0)
+        grads_ref[p] = nt(pick, dfeats[...]).astype(BF).reshape(3, atoms, rows)
+        both = [
+            remote(grads_ref.at[p, 1], landed.at[p, 1], back_sem, (s, 0), (lower, ch)),
+            remote(grads_ref.at[p, 2], landed.at[p, 0], back_sem, (s, 1), (upper, ch)),
+        ]
+        for copy in both:
+            copy.start()
+        homeward.append((s, p, both))
+
+    flat[...] = nt(spread_f, agg_ref[...])
+    for k in range(count):
+        mine_k = node_ref[k].astype(F32) + flat[:, k * group : (k + 1) * group]
+        updated_ref[k] = mine_k.astype(BF)
+
+    last = []
+    for s, p, both in homeward:
+        for copy in both:
+            copy.wait_recv()
+        total = (
+            grads_ref[p, 0].astype(F32)
+            + landed[p, 0].astype(F32)
+            + landed[p, 1].astype(F32)
+        )
+        if s > 0:
+            partial[s - 1] = total.astype(BF)
+            copy = remote(partial.at[s - 1], sums.at[s - 1], sum_sem, (s,), (dom, p))
+            copy.start()
+            last.append(copy)
+    for copy in last:
+        copy.wait_recv()
+    for s in range(1, n_ch):
+        total = total + sums[s - 1].astype(F32)
+    flat[...] = total
+    for k in range(count):
+        out_ref[k] = cot_ref[k].astype(F32) + flat[:, k * group : (k + 1) * group]
+    for copy in across + along + [c for h in homeward for c in h[2]] + last:
+        copy.wait_send()
 
 
 def on_device(
@@ -367,28 +416,28 @@
     edges = slots * atoms
     rows = count * group
     vmem = pl.BlockSpec(memory_space=VMEM)
-    blocks = jax.ShapeDtypeStruct((n_ch, 3, atoms, rows), BF)
-    sems = [
-        pltpu.SemaphoreType.DMA((n_ch, 3)),
-        pltpu.SemaphoreType.DMA((n_ch, 3)),
-        pltpu.SemaphoreType.DMA,
-    ]
-    table = pl.pallas_call(
-        functools.partial(share_kernel, n_dom, n_ch),
-        out_shape=blocks,
-        in_specs=[vmem],
-        out_specs=vmem,
-        scratch_shapes=[VMEM((atoms, rows), BF)] + sems,
-        compiler_params=pltpu.CompilerParams(collective_id=0, has_side_effects=True),
-        name="share",
-    )(node_irreps)
+    anywhere = pl.BlockSpec(memory_space=pl.ANY)
     n_pairs = sum(len(b[3]) for b in BLOCKS)
-    updated, grads = pl.pallas_call(
-        functools.partial(work_kernel, chans // HEADS),
-        out_shape=(jax.ShapeDtypeStruct(node_irreps.shape, BF), blocks),
-        in_specs=[vmem] * 12,
+    dma = pltpu.SemaphoreType.DMA
+    flipped = (count, atoms, group)
+    updated, irreps_grad = pl.pallas_call(
+        functools.partial(kernel, n_dom, n_ch, chans // HEADS),
+        out_shape=(jax.ShapeDtypeStruct(flipped, BF), jax.ShapeDtypeStruct(flipped, F32)),
+        in_specs=[vmem] * 6 + [anywhere] * 5,
         out_specs=(vmem, vmem),
         scratch_shapes=[
+            VMEM(flipped, BF),
+            VMEM(wigner.shape, F32),
+            VMEM((LMAX + 1, group, (LMAX + 1) * chans), BF),
+            VMEM((2, LMAX, group, LMAX * chans), BF),
+            VMEM((2, LMAX - 1, group, (LMAX - 1) * chans), BF),
+            VMEM((n_ch, 3, atoms, rows), BF),
+            VMEM((n_ch, 3, atoms, rows), BF),
+            VMEM((n_ch, 2, atoms, rows), BF),
+            VMEM((max(n_ch - 1, 1), atoms, rows), BF),
+            VMEM((max(n_ch - 1, 1), atoms, rows), BF),
+            VMEM((atoms, rows), F32),
+            VMEM((atoms, rows), BF),
             VMEM((wigner.shape[0], edges), F32),
             VMEM((n_ch * rows, edges), F32),
             VMEM(((LMAX + 1) * chans, edges), BF),
@@ -398,33 +447,31 @@
             VMEM((rows, edges), F32),
             VMEM((n_pairs * group, edges), BF),
             VMEM((rows, edges), BF),
+            VMEM((rows, edges), BF),
+            dma((2 + 3 * LMAX,)),
+            dma((2, n_ch)),
+            dma((2, n_ch, 2)),
+            dma((2, n_ch, 2)),
+            dma((2, n_ch)),
         ],
-        compiler_params=pltpu.CompilerParams(vmem_limit_bytes=56 * 1024 * 1024),
-        name="work",
+        compiler_params=pltpu.CompilerParams(
+            collective_id=0, has_side_effects=True, vmem_limit_bytes=56 * 1024 * 1024
+        ),
+        name="layer",
     )(
-        table,
-        node_irreps,
-        out_grad,
+        jnp.transpose(node_irreps, (0, 2, 1)),
         edge_source,
         edge_rotation,
         edge_count.reshape(1, atoms),
         ghost_slot.reshape(1, -1),
+        attn_vector.reshape(1, group),
+        jnp.transpose(out_grad, (0, 2, 1)),
         wigner,
-        so2_m0.reshape((LMAX + 1) * group, (LMAX + 1) * chans),
-        so2_m1.reshape(2 * LMAX * group, LMAX * chans),
-        so2_m2.reshape(2 * (LMAX - 1) * group, (LMAX - 1) * chans),
-        attn_vector.reshape(1, group),
+        jnp.transpose(so2_m0, (0, 2, 1, 3)),
+        jnp.transpose(so2_m1, (0, 1, 3, 2, 4)),
+        jnp.transpose(so2_m2, (0, 1, 3, 2, 4)),
     )
-    irreps_grad = pl.pallas_call(
-        functools.partial(return_kernel, n_dom, n_ch),
-        out_shape=jax.ShapeDtypeStruct(node_irreps.shape, F32),
-        in_specs=[vmem, vmem],
-        out_specs=vmem,
-        scratch_shapes=[VMEM(blocks.shape, BF)] + sems,
-        compiler_params=pltpu.CompilerParams(collective_id=1, has_side_effects=True),
-        name="give_back",
-    )(grads, out_grad)
-    return (updated, irreps_grad)
+    return (jnp.transpose(updated, (0, 2, 1)), jnp.transpose(irreps_grad, (0, 2, 1)))
 
 
 def solution(mesh):

time: 51.6 us -> 35 us (0.68)
  local copies, waits for them, and re-layouts: 12.7 us -> 3.39 us
  Pallas kernels: 38 us -> 30.7 us
    unnamed x20 -> x2, local copies, waits for them, and re-layouts: 12.7 us -> 3.39 us
    pallas_call x3 -> x1, Pallas kernels: 38 us -> 30.7 us  [on_device(): pl.pallas_call(functools.partial(kernel, n_dom, n_ch, chans // HEADS), ou...]
where the time goes in v1:
time: 35 us; the launch traced here: 34.8 us
  Pallas kernels  30.7 us (88%)
  local copies, waits for them, and re-layouts  3.39 us (10%)
  between operations  0.64 us (2%)
    pallas_call x1, Pallas kernels, on_device(): pl.pallas_call(functools.partial(kernel, n_dom, n_ch, chans // HEADS), ou...  30.7 us
    unnamed x2, local copies, waits for them, and re-layouts  3.39 us

profile of v1, /device:TPU:0, one launch (start us, length us, event | category | flops | bytes accessed | tf_op | source)
XLA Modules:
  0.0 34.8 jit_solution(4513516256437720788)
XLA Ops:
  0.6 30.7 %layer.1 = (bf16[49,16,64]{2,1,0:T(8,128)(2,1)}, f32[49,16,64]{2,1,0:T(8,128)}) custom-call(bf16[49,16,64]{2,1,0:T(8,128)(2,1)} %bitcast.14, s32[8,16]{1,0:T(8,128)} %source_ref.1, s32[8,16]{1,0:T(8,128)} %turn_ref.1, s32[1,16]{1,0:T(1,128)} %bitcast.17, s32[1,16]{1,0:T(1,128)} %bitcast.18, f32[1,64]{1,0:T(1,128)} %bitcast.19, bf16[49,16,64]{2,1,0:T(8,128)(2,1)} %bitcast.15, ...), custom_call_target="tpu_custom_call" | custom-call | tf_op jit(solution)/shard_map/layer/pallas_call | solution.py:423
  31.4 1.6 %copy.15 = bf16[49,64,16]{1,2,0:T(8,128)(2,1)} copy(bf16[49,64,16]{1,2,0:T(8,128)(2,1)} %bitcast.16) | data formatting | bytes 200704
  33.0 1.8 %copy.16 = f32[49,64,16]{1,2,0:T(8,128)} copy(f32[49,64,16]{1,2,0:T(8,128)} %bitcast.13) | data formatting | bytes 401408
